TPU v7x, 32 devices: a whole 2x2x4 slice. The times are simulated.
32 devices in a mesh: shard: 8 (over z, y), tensor: 4 (over x, core).
Axes of the slice: x: 2, y: 2, z: 4, core: 2. Of those that a mesh axis runs over, the one named last changes fastest.
Arguments:
- grad_parts: float32 [4, 4, 768, 768], P('tensor', None, 'shard'), may hold values from -0.6 to 0.6
- adam_v: float32 [4, 768, 768], P(None, 'shard', 'tensor'), may hold values from 0.01 to 0.2
- left_stat: float32 [8, 768, 768], P('shard', 'tensor'), may hold values from -6 to 6
- right_stat: float32 [8, 768, 768], P('shard', 'tensor'), may hold values from -6 to 6
- left_root: bfloat16 [8, 768, 768], P('shard', 'tensor'), as said below
- right_root: bfloat16 [8, 768, 768], P('shard', 'tensor'), as said below
- owner: int32 [4], replicated, may hold values from 0 to 7, as said below
- vec_parts: float32 [4, 4, 768], P('tensor', None, 'shard'), may hold values from -0.6 to 0.6
- vec_m: float32 [4, 768], P(None, 'shard'), may hold values from -0.3 to 0.3
- vec_v: float32 [4, 768], P(None, 'shard'), may hold values from 0.01 to 0.2
Outputs:
- update: float32 [4, 768, 768], P(None, 'shard', 'tensor')
- new_adam_v: float32 [4, 768, 768], P(None, 'shard', 'tensor')
- new_left: float32 [8, 768, 768], P('shard', 'tensor')
- new_right: float32 [8, 768, 768], P('shard', 'tensor')
- new_vec_m: float32 [4, 768], P(None, 'shard')
- new_vec_v: float32 [4, 768], P(None, 'shard')
- vec_step: float32 [4, 768], P(None, 'shard')
Inputs may be any that keep to these rules, and one draw needn't show every extreme that they name: owner holds 4 distinct slot numbers: no slot owns two tiles. `left_root`: each slot's matrix is symmetric. `right_root`: each slot's matrix is symmetric.
All inputs are finite; a program needn't handle non-finite values.
Results may differ from a plain program's by a relative error of at most 0.0003.
Values may be sent and summed in bfloat16 or wider, within the bound.
No kernel may reach another device: no remote copies, remote signals or barrier semaphores. Data moves between devices by JAX's collectives and lax.ppermute only.
A program may use at most 64 MiB of HBM per device.

v0:
```python
import jax
import jax.numpy as jnp
from jax import lax
from jax.sharding import PartitionSpec as P

BETA_ONE = 0.9
BETA_TWO = 0.95
STAT_DECAY = 0.95
STEP_COUNT = 10.0
EPSILON = 1e-08
NORM_EPS = 1e-06
HIGH = lax.Precision.HIGHEST


def local(
    grad_parts, adam_v, left_stat, right_stat, left_root, right_root, owner, vec_parts, vec_m, vec_v
):
    shards = lax.axis_size("shard")
    tiles = owner.shape[0]
    grad = lax.psum_scatter(grad_parts[0], "tensor", scatter_dimension=2, tiled=True)
    rows_dev = grad.shape[1]
    cols_dev = grad.shape[2]
    new_adam_v = BETA_TWO * adam_v + (1.0 - BETA_TWO) * grad * grad
    bias_two = 1.0 - BETA_TWO**STEP_COUNT
    adam_dir = grad / (jnp.sqrt(new_adam_v / bias_two) + EPSILON)
    adam_sq = jnp.sum(adam_dir * adam_dir, axis=(1, 2))
    vec_grad = lax.psum(vec_parts[0], "tensor")
    new_vec_m = BETA_ONE * vec_m + (1.0 - BETA_ONE) * vec_grad
    new_vec_v = BETA_TWO * vec_v + (1.0 - BETA_TWO) * vec_grad * vec_grad
    bias_one = 1.0 - BETA_ONE**STEP_COUNT
    vec_step = new_vec_m / bias_one / (jnp.sqrt(new_vec_v / bias_two) + EPSILON)
    slot_hot = (jnp.arange(shards, dtype=jnp.int32)[:, None] == owner[None, :]).astype(jnp.float32)
    outgoing = jnp.dot(slot_hot, grad.reshape(tiles, rows_dev * cols_dev), precision=HIGH)
    outgoing = outgoing.reshape(shards, rows_dev, cols_dev)
    arrived = lax.all_to_all(outgoing, "shard", split_axis=0, concat_axis=1, tiled=True)[0]
    whole = lax.all_gather(arrived, "tensor", axis=1, tiled=True)
    start = lax.axis_index("tensor") * cols_dev
    tile_rows = lax.dynamic_slice_in_dim(whole, start, cols_dev, 0)
    new_left = STAT_DECAY * left_stat[0] + (1.0 - STAT_DECAY) * jnp.dot(
        tile_rows, whole.T, precision=HIGH
    )
    new_right = STAT_DECAY * right_stat[0] + (1.0 - STAT_DECAY) * jnp.dot(
        arrived.T, whole, precision=HIGH
    )
    right_full = lax.all_gather(right_root[0], "tensor", axis=0, tiled=True).astype(jnp.float32)
    left_part = jnp.dot(left_root[0].astype(jnp.float32), whole, precision=HIGH)
    row_block = jnp.dot(left_part, right_full, precision=HIGH)
    direction = lax.all_to_all(row_block[None], "tensor", split_axis=2, concat_axis=1, tiled=True)[
        0
    ]
    returned = lax.all_to_all(
        direction.reshape(shards, rows_dev, cols_dev),
        "shard",
        split_axis=0,
        concat_axis=0,
        tiled=True,
    )
    update = jnp.dot(slot_hot.T, returned.reshape(shards, rows_dev * cols_dev), precision=HIGH)
    update = update.reshape(tiles, rows_dev, cols_dev)
    shampoo_local = jnp.sum(update * update, axis=(1, 2))
    adam_total, shampoo_total = lax.psum((adam_sq, shampoo_local), ("shard", "tensor"))
    graft = jnp.sqrt(adam_total) / (jnp.sqrt(shampoo_total) + NORM_EPS)
    update = graft[:, None, None] * update
    return (update, new_adam_v, new_left[None], new_right[None], new_vec_m, new_vec_v, vec_step)


def solution(mesh):
    in_specs = (
        P("tensor", None, "shard", None),
        P(None, "shard", "tensor"),
        P("shard", "tensor", None),
        P("shard", "tensor", None),
        P("shard", "tensor", None),
        P("shard", "tensor", None),
        P(),
        P("tensor", None, "shard"),
        P(None, "shard"),
        P(None, "shard"),
    )
    out_specs = (
        P(None, "shard", "tensor"),
        P(None, "shard", "tensor"),
        P("shard", "tensor", None),
        P("shard", "tensor", None),
        P(None, "shard"),
        P(None, "shard"),
        P(None, "shard"),
    )
    return jax.shard_map(local, mesh=mesh, in_specs=in_specs, out_specs=out_specs, check_vma=False)
```

profile of v0, /device:TPU:0, one launch (start us, length us, event | category | flops | bytes accessed | tf_op | source)
XLA Modules:
  0.0 205.5 jit_solution(14201237901707531373)
XLA Ops:
  7.2 0.0 copy-start
  7.2 0.0 reduce-scatter.4.cloned.1.call-start
  7.2 1.8 copy.38
  9.0 1.8 reshape.39
  10.8 0.0 copy-start.4
  10.8 0.0 reduce-scatter.4.cloned.1.call-update
  10.8 0.0 all-gather.4.cloned.1.call-start
  10.9 28.5 %reduce-scatter.4.cloned.1.call-done = f32[192,384]{1,0:T(8,128)} async-done(((f32[768,384]{1,0:T(8,128)}), f32[192,384]{1,0:T(8,128)}) %reduce-scatter.4.cloned.1.call-update) | async-done | bytes 294928
  39.4 1.2 reshape.40
  40.6 0.2 copy.39
  40.9 0.0 copy-start.2
  40.9 0.2 reshape.35
  41.1 0.2 dot_general.27
  41.3 0.0 copy-done.4
  41.4 0.8 fusion.9
  42.2 0.0 copy-done.2
  42.2 0.3 copy.30
  42.4 25.5 %all_to_all.29 = f32[8,96,192]{2,1,0:T(8,128)S(1)} all-to-all(f32[8,96,192]{2,1,0:T(8,128)S(1)} %copy.30), channel_id=1, replica_groups=mesh['shard'=8,'tensor'=4] {'shard'}, dimensions={0} | all-to-all | bytes 1179648 | tf_op jit(solution)/shard_map/all_to_all | solution.py:35
  67.9 1.1 copy.37
  69.0 0.0 all-gather.4.cloned.1.call-update
  69.0 0.0 all-gather.6.cloned.1.call-start
  69.1 0.7 all-gather.6.cloned.1.call-update
  69.7 21.6 %all-gather.4.cloned.1.call-done = f32[768,768]{0,1:T(8,128)} async-done(((f32[768,192]{0,1:T(8,128)}), f32[768,768]{0,1:T(8,128)}) %all-gather.4.cloned.1.call-update) | async-done | bytes 2359312 | tf_op jit(solution)/shard_map/all_gather | solution.py:36
  91.3 0.0 copy-done
  91.3 3.1 %fusion.11 = f32[768,192]{0,1:T(8,128)S(1)} fusion(f32[768,768]{0,1:T(8,128)} %all-gather.4.cloned.1.call-done, bf16[1,192,768]{2,1,0:T(8,128)(2,1)S(1)} %copy-done), kind=kOutput, calls=%fused_computation.17 | convolution fusion | flops 1358954496 | bytes 3244032 | tf_op jit(solution)/shard_map/dot_general | solution.py:46
  94.4 16.0 %all-gather.6.cloned.1.call-done = bf16[1,768,768]{2,1,0:T(8,128)(2,1)} async-done(((bf16[1,192,768]{2,1,0:T(8,128)(2,1)}), bf16[1,768,768]{2,1,0:T(8,128)(2,1)}) %all-gather.6.cloned.1.call-update) | async-done | bytes 1179664 | tf_op jit(solution)/shard_map/all_gather | solution.py:45
  110.4 2.1 %convolution_bitcast_fusion = f32[1,192,768]{2,1,0:T(8,128)S(1)} fusion(f32[768,192]{0,1:T(8,128)S(1)} %fusion.11, bf16[1,768,768]{2,1,0:T(8,128)(2,1)} %all-gather.6.cloned.1.call-done), kind=kOutput, calls=%fused_computation.6 | convolution fusion | flops 1358954496 | bytes 2359296 | tf_op jit(solution)/shard_map/dot_general | solution.py:47
  112.6 0.6 copy.32
  113.2 14.1 %all_to_all.30 = f32[1,192,768]{1,0,2:T(1,128)S(1)} all-to-all(f32[1,192,768]{1,0,2:T(1,128)S(1)} %copy.32), channel_id=1, replica_groups=mesh['shard'=8,'tensor'=4] {'tensor'}, dimensions={2} | all-to-all | bytes 1179648 | tf_op jit(solution)/shard_map/all_to_all | solution.py:48
  127.2 0.4 copy.33
  127.7 0.0 copy-start.5
  127.7 0.0 copy-start.6
  127.7 0.0 copy-start.7
  127.7 1.5 all_to_all.23
  129.2 0.0 copy-start.1
  129.2 2.3 %copy.34 = f32[1,4,192,192]{3,2,1,0:T(8,128)} copy(f32[1,4,192,192]{3,1,2,0:T(4,128)} %bitcast.44) | data formatting | bytes 1179648 | tf_op jit(solution)/shard_map/all_to_all | solution.py:48
  131.5 5.5 %all-to-all-start.2 = ((f32[8,96,192]{2,1,0:T(8,128)}), f32[8,96,192]{2,1,0:T(8,128)}, u32[]{:S(2)}, u32[]{:S(2)}) async-start(f32[8,96,192]{2,1,0:T(8,128)} %bitcast.43), calls=%async_computation.2 | async-start | bytes 1572864 | tf_op jit(solution)/shard_map/all_to_all | solution.py:51
  137.0 0.0 copy-done.5
  137.0 6.2 %psum.23 = f32[4,96]{1,0:T(4,128)S(1)} all-reduce(f32[4,96]{1,0:T(4,128)S(1)} %bitcast.49), channel_id=1, replica_groups=mesh['shard'=8,'tensor'=4] {'tensor'}, use_global_device_ids=true, to_apply=%region_5.0 | all-reduce | flops 384 | bytes 3072 | tf_op jit(solution)/shard_map/psum | solution.py:27
  143.3 0.0 copy-done.6
  143.3 0.0 copy-done.7
  143.3 0.6 add_divide_fusion
  143.9 0.0 copy-start.3
  143.9 2.1 %multiply_reduce_fusion.1 = (f32[4]{0:T(128)S(1)}, f32[4,96,192]{2,1,0:T(8,128)}) fusion(f32[4,96,192]{2,1,0:T(8,128)} %copy-done.2, f32[4,96,192]{2,1,0:T(8,128)} %param.11), kind=kLoop, calls=%fused_computation.16 | loop fusion | flops 663548 | bytes 884752 | tf_op jit(solution)/shard_map/reduce_sum | solution.py:26
  146.0 0.0 copy-done.1
  146.0 4.0 %fusion.3 = f32[1,192,768]{2,1,0:T(8,128)} fusion(f32[768,768]{0,1:T(8,128)S(1)} %copy-done.1, s32[]{:T(128)S(6)} %select_n.3, f32[1,192,768]{2,1,0:T(8,128)} %param.12), kind=kOutput, calls=%fused_computation.5 | convolution fusion | flops 1359396864 | bytes 4325380 | tf_op jit(solution)/shard_map/dot_general | solution.py:39
  150.0 0.0 copy-done.3
  150.0 4.8 %fusion.1 = f32[1,192,768]{2,1,0:T(8,128)} fusion(f32[768,192]{1,0:T(8,128)S(1)} %bitcast.41, f32[768,768]{0,1:T(8,128)S(1)} %copy-done.1, f32[1,192,768]{2,1,0:T(8,128)S(1)} %copy-done.3), kind=kOutput, calls=%fused_computation.2 | convolution fusion | flops 1359396864 | bytes 4128768 | tf_op jit(solution)/shard_map/dot_general | solution.py:42
  154.8 2.2 %all-to-all-done.2 = f32[8,96,192]{2,1,0:T(8,128)} async-done(((f32[8,96,192]{2,1,0:T(8,128)}), f32[8,96,192]{2,1,0:T(8,128)}, u32[]{:S(2)}, u32[]{:S(2)}) %all-to-all-start.2) | async-done | bytes 589856 | tf_op jit(solution)/shard_map/all_to_all | solution.py:51
  157.0 1.4 reshape.36
  158.5 0.3 dot_general.32
  158.8 1.1 multiply_reduce_fusion
  159.9 38.0 %all-reduce = (f32[4]{0:T(128)S(1)}, f32[4]{0:T(128)S(1)}) all-reduce(f32[4]{0:T(128)S(1)} %get-tuple-element.42, f32[4]{0:T(128)S(1)} %get-tuple-element.40), channel_id=1, replica_groups=mesh['shard'=8,'tensor'=4] {'shard','tensor'}, use_global_device_ids=true, to_apply=%region_4.0 | all-reduce | flops 8 | bytes 64 | tf_op jit(solution)/shard_map/psum | solution.py:61
  198.0 0.1 broadcast_multiply_fusion
  198.1 0.8 copy.36
  (1 shorter events, 0.0 us)
Async XLA Ops:
  7.2 84.1 %copy-start = (bf16[1,192,768]{2,1,0:T(8,128)(2,1)S(1)}, bf16[1,192,768]{2,1,0:T(8,128)(2,1)}, u32[]{:S(2)}) copy-start(bf16[1,192,768]{2,1,0:T(8,128)(2,1)} %param.14) | copy-start | bytes 884740
  7.2 32.2 %reduce-scatter.4.cloned.1.call-start = ((), (), s32[]{:S(2)}) async-start(), calls=%async_computation.6 | async-start | bytes 1474560
  10.8 30.5 %copy-start.4 = (s32[4]{0:T(128)S(1)}, s32[4]{0:T(128)}, u32[]{:S(2)}) copy-start(s32[4]{0:T(128)} %param.16) | copy-start | bytes 52
  10.8 80.5 %all-gather.4.cloned.1.call-start = ((), (), s32[]{:S(2)}) async-start(), calls=%async_computation.4 | async-start | bytes 2949120 | tf_op jit(solution)/shard_map/all_gather | solution.py:36
  40.9 1.3 copy-start.2
  69.0 41.4 %all-gather.6.cloned.1.call-start = ((), (), s32[]{:S(2)}) async-start(), calls=%async_computation.5 | async-start | bytes 1474560 | tf_op jit(solution)/shard_map/all_gather | solution.py:45
  127.7 9.3 %copy-start.5 = (f32[1,4,96]{2,1,0:T(4,128)S(1)}, f32[1,4,96]{2,1,0:T(4,128)}, u32[]{:S(2)}) copy-start(f32[1,4,96]{2,1,0:T(4,128)} %param.17) | copy-start | bytes 4612
  127.7 15.6 %copy-start.6 = (f32[4,96]{1,0:T(4,128)S(1)}, f32[4,96]{1,0:T(4,128)}, u32[]{:S(2)}) copy-start(f32[4,96]{1,0:T(4,128)} %param.19) | copy-start | bytes 4612
  127.7 15.6 %copy-start.7 = (f32[4,96]{1,0:T(4,128)S(1)}, f32[4,96]{1,0:T(4,128)}, u32[]{:S(2)}) copy-start(f32[4,96]{1,0:T(4,128)} %param.18) | copy-start | bytes 4612
  129.2 16.8 %copy-start.1 = (f32[768,768]{0,1:T(8,128)S(1)}, f32[768,768]{0,1:T(8,128)}, u32[]{:S(2)}) copy-start(f32[768,768]{0,1:T(8,128)} %all-gather.4.cloned.1.call-done) | copy-start | bytes 7077892
  131.5 25.5 %all-to-all-start.2 = ((f32[8,96,192]{2,1,0:T(8,128)}), f32[8,96,192]{2,1,0:T(8,128)}, u32[]{:S(2)}, u32[]{:S(2)}) async-start(f32[8,96,192]{2,1,0:T(8,128)} %bitcast.43), calls=%async_computation.2 | async-start | bytes 1572864 | tf_op jit(solution)/shard_map/all_to_all | solution.py:51
  143.9 6.1 %copy-start.3 = (f32[1,192,768]{2,1,0:T(8,128)S(1)}, f32[1,192,768]{2,1,0:T(8,128)}, u32[]{:S(2)}) copy-start(f32[1,192,768]{2,1,0:T(8,128)} %param.13) | copy-start | bytes 1769476
Sparse Core Ops, SparseCore 0:
  11.0 28.4 reduce-scatter.3
  69.1 22.1 all-gather.3
  93.0 17.4 all-gather.5
where the time goes:
time: 206 us; the launch traced here: 205 us
  blocking collectives  83.8 us (41%)
  waiting for transfers between devices  69.1 us (34%)
  matrix products  16 us (8%)
  local copies, waits for them, and re-layouts  14.2 us (7%)
  between operations  13.9 us (7%)
  starting transfers between devices  5.64 us (3%)
  other arithmetic  2.89 us (1%)
    psum x1, blocking collectives, local(): lax.psum((adam_sq, shampoo_local), ('shard', 'tensor'))  38 us
    unnamed x4, waiting for transfers between devices  29.3 us
    all_to_all x1, blocking collectives, local(): lax.all_to_all(outgoing, 'shard', split_axis=0, concat_axis=1, tiled=True)  25.5 us
    all_gather x1, waiting for transfers between devices, local(): whole = lax.all_gather(arrived, 'tensor', axis=1, tiled=True)  21.6 us
    all_gather x1, waiting for transfers between devices, local(): lax.all_gather(right_root[0], 'tensor', axis=0, tiled=True)  16 us
    all_to_all x1, blocking collectives, local(): lax.all_to_all(row_block[None], 'tensor', split_axis=2, concat_axis=1, ti...  14.1 us
    psum x1, blocking collectives, local(): vec_grad = lax.psum(vec_parts[0], 'tensor')  6.25 us
    unnamed x21, local copies, waits for them, and re-layouts  5.86 us
  transfers between devices with their start and end apart: 4, of which 4 were waited for; matrix products, arithmetic and copies ran while one was open for 7% of the time, Pallas kernels for 0%

commit v1 on v0

--- a/solution.py
+++ b/solution.py
@@ -10,6 +10,21 @@
 EPSILON = 1e-08
 NORM_EPS = 1e-06
 HIGH = lax.Precision.HIGHEST
+
+
+def update_thing_up(vector, shard_axis, array_axis):
+    answer = lax.axis_size(shard_axis)
+    local_out, o_now = (answer, lax.axis_index(shard_axis))
+    y, q_next = (vector, 1)
+    while q_next < local_out:
+        ready = lax.ppermute(
+            y, axis_name=shard_axis, perm=[(src_i, src_i ^ q_next) for src_i in range(local_out)]
+        )
+        m_next = jnp.concatenate([y, ready], axis=array_axis)
+        b_now = jnp.concatenate([ready, y], axis=array_axis)
+        y = jnp.where(o_now & q_next == 0, m_next, b_now)
+        q_next = 2 * q_next
+    return y
 
 
 def local(
@@ -33,7 +48,7 @@
     outgoing = jnp.dot(slot_hot, grad.reshape(tiles, rows_dev * cols_dev), precision=HIGH)
     outgoing = outgoing.reshape(shards, rows_dev, cols_dev)
     arrived = lax.all_to_all(outgoing, "shard", split_axis=0, concat_axis=1, tiled=True)[0]
-    whole = lax.all_gather(arrived, "tensor", axis=1, tiled=True)
+    whole = update_thing_up(arrived, "tensor", 1)
     start = lax.axis_index("tensor") * cols_dev
     tile_rows = lax.dynamic_slice_in_dim(whole, start, cols_dev, 0)
     new_left = STAT_DECAY * left_stat[0] + (1.0 - STAT_DECAY) * jnp.dot(

time: 206 us -> 213 us (1.034)
  local copies, waits for them, and re-layouts: 14.2 us -> 19.6 us
  other arithmetic: 2.89 us -> 5.68 us
  waiting for transfers between devices: 69.1 us -> 66.4 us
    ppermute x0 -> x2, waiting for transfers between devices: none -> 35.4 us  [update_thing_up(): lax.ppermute(y, axis_name=shard_axis, perm=[(src_i, src_i ^ q_next) for s...]
    all_gather x1 -> x0, waiting for transfers between devices: 21.6 us -> none  [local(): whole = lax.all_gather(arrived, 'tensor', axis=1, tiled=True)]
    all_gather x1, waiting for transfers between devices: 16 us -> 0.01 us  [local(): lax.all_gather(right_root[0], 'tensor', axis=0, tiled=True)]
    all_to_all x3, local copies, waits for them, and re-layouts: 4.23 us -> 7.64 us  [local(): lax.all_to_all(row_block[None], 'tensor', split_axis=2, concat_axis=1, ti...]
    select_n x0 -> x2, other arithmetic: none -> 2.79 us  [update_thing_up(): y = jnp.where(o_now & q_next == 0, m_next, b_now)]
    broadcast_in_dim x1, local copies, waits for them, and re-layouts: 0.58 us -> 2.99 us  [local(): row_block[None]]
    unnamed x4 -> x3, waiting for transfers between devices: 29.3 us -> 28.6 us
  transfers between devices with their start and end apart: 4 -> 5, of which waited for: 4 -> 4; matrix products, arithmetic and copies ran while one was open for 7% -> 8% of each run, Pallas kernels for 0% -> 0%
where the time goes in v1:
time: 213 us
  blocking collectives  85.6 us (40%)
  waiting for transfers between devices  66.4 us (31%)
  local copies, waits for them, and re-layouts  19.6 us (9%)
  matrix products  16.1 us (8%)
  between operations  14.2 us (7%)
  other arithmetic  5.68 us (3%)
  starting transfers between devices  4.98 us (2%)
    psum x1, blocking collectives, local(): lax.psum((adam_sq, shampoo_local), ('shard', 'tensor'))  38 us
    ppermute x2, waiting for transfers between devices, update_thing_up(): lax.ppermute(y, axis_name=shard_axis, perm=[(src_i, src_i ^ q_next) for s...  35.4 us
    unnamed x3, waiting for transfers between devices  28.6 us
    all_to_all x1, blocking collectives, local(): lax.all_to_all(outgoing, 'shard', split_axis=0, concat_axis=1, tiled=True)  25.5 us
    all_to_all x1, blocking collectives, local(): lax.all_to_all(row_block[None], 'tensor', split_axis=2, concat_axis=1, ti...  15.9 us
    all_to_all x3, local copies, waits for them, and re-layouts, local(): lax.all_to_all(row_block[None], 'tensor', split_axis=2, concat_axis=1, ti...  7.64 us
    unnamed x21, local copies, waits for them, and re-layouts  6.25 us
    psum x1, blocking collectives, local(): vec_grad = lax.psum(vec_parts[0], 'tensor')  6.25 us
  transfers between devices with their start and end apart: 5, of which 4 were waited for; matrix products, arithmetic and copies ran while one was open for 8% of the time, Pallas kernels for 0%

profile of v1, /device:TPU:0, one launch (start us, length us, event | category | flops | bytes accessed | tf_op | source)
XLA Modules:
  0.0 212.6 jit_solution(12833048876046035035)
XLA Ops:
  7.2 0.0 copy-start
  7.2 0.0 reduce-scatter.4.cloned.1.call-start
  7.2 1.8 copy.38
  9.0 1.8 reshape.39
  10.8 0.0 copy-start.4
  10.8 0.0 reduce-scatter.4.cloned.1.call-update
  10.8 0.0 all-gather.3.cloned.1.call-start
  10.9 28.5 %reduce-scatter.4.cloned.1.call-done = f32[192,384]{1,0:T(8,128)} async-done(((f32[768,384]{1,0:T(8,128)}), f32[192,384]{1,0:T(8,128)}) %reduce-scatter.4.cloned.1.call-update) | async-done | bytes 294928
  39.4 1.2 reshape.40
  40.6 0.2 copy.39
  40.8 0.0 copy-start.2
  40.9 0.2 reshape.35
  41.1 0.2 dot_general.27
  41.3 0.0 copy-done.4
  41.3 0.8 fusion.9
  42.2 0.0 copy-done.2
  42.2 0.3 copy.30
  42.4 25.5 %all_to_all.29 = f32[8,96,192]{2,1,0:T(8,128)S(1)} all-to-all(f32[8,96,192]{2,1,0:T(8,128)S(1)} %copy.30), channel_id=1, replica_groups=mesh['shard'=8,'tensor'=4] {'shard'}, dimensions={0} | all-to-all | bytes 1179648 | tf_op jit(solution)/shard_map/all_to_all | solution.py:50
  67.9 0.2 copy.37
  68.2 0.1 collective-permute-start
  68.2 0.0 all-gather.3.cloned.1.call-update
  68.3 2.0 collective-permute-done
  70.2 0.1 maximum_select_fusion.1
  70.3 0.0 copy-start.1
  70.3 0.6 collective-permute-start.1
  70.9 0.4 copy-done.1
  71.4 33.5 %collective-permute-done.1 = f32[768,384]{0,1:T(8,128)} collective-permute-done((f32[768,384]{0,1:T(8,128)S(1)}, f32[768,384]{0,1:T(8,128)}, u32[]{:S(2)}, u32[]{:S(2)}) %collective-permute-start.1) | collective-permute-done | bytes 1179680 | tf_op jit(solution)/shard_map/ppermute | solution.py:20
  104.8 2.7 %maximum_select_fusion = f32[768,768]{0,1:T(8,128)S(1)} fusion(f32[768,384]{0,1:T(8,128)} %collective-permute-done.1, f32[768,384]{0,1:T(8,128)} %copy-done.1, pred[]{:T(512)S(6)} %eq.22), kind=kLoop, calls=%fused_computation | loop fusion | flops 1769472 | bytes 4718593 | tf_op jit(solution)/shard_map/jit(_where)/select_n | solution.py:25
  107.5 0.0 copy-done
  107.5 2.3 %fusion.11 = f32[768,192]{0,1:T(8,128)} fusion(f32[768,768]{0,1:T(8,128)S(1)} %maximum_select_fusion, bf16[1,192,768]{2,1,0:T(8,128)(2,1)S(1)} %copy-done), kind=kOutput, calls=%fused_computation.19 | convolution fusion | flops 1358954496 | bytes 3244032 | tf_op jit(solution)/shard_map/dot_general | solution.py:61
  109.8 0.0 all-gather.3.cloned.1.call-done
  109.8 3.1 %convolution_bitcast_fusion = f32[1,192,768]{2,1,0:T(8,128)} fusion(f32[768,192]{0,1:T(8,128)} %fusion.11, bf16[1,768,768]{2,1,0:T(8,128)(2,1)} %all-gather.3.cloned.1.call-done), kind=kOutput, calls=%fused_computation.7 | convolution fusion | flops 1358954496 | bytes 2359296 | tf_op jit(solution)/shard_map/dot_general | solution.py:62
  113.0 3.0 %copy.32 = f32[1,192,768]{1,0,2:T(1,128)} copy(f32[1,192,768]{2,1,0:T(8,128)} %convolution_bitcast_fusion) | data formatting | bytes 1179648 | tf_op jit(solution)/shard_map/broadcast_in_dim | solution.py:63
  115.9 15.9 %all_to_all.30 = f32[1,192,768]{1,0,2:T(1,128)} all-to-all(f32[1,192,768]{1,0,2:T(1,128)} %copy.32), channel_id=1, replica_groups=mesh['shard'=8,'tensor'=4] {'tensor'}, dimensions={2} | all-to-all | bytes 1179648 | tf_op jit(solution)/shard_map/all_to_all | solution.py:63
  131.9 2.9 %copy.33 = f32[1,192,768]{2,1,0:T(8,128)} copy(f32[1,192,768]{1,0,2:T(1,128)} %all_to_all.30) | data formatting | bytes 1179648 | tf_op jit(solution)/shard_map/all_to_all | solution.py:63
  134.8 0.0 copy-start.5
  134.8 0.0 copy-start.6
  134.8 0.0 copy-start.7
  134.8 2.6 %all_to_all.23 = f32[1,192,4,192]{3,2,1,0:T(4,128)} reshape(f32[1,192,768]{2,1,0:T(8,128)} %copy.33) | data formatting | bytes 1179648 | tf_op jit(solution)/shard_map/all_to_all | solution.py:63
  137.3 2.2 %copy.34 = f32[1,4,192,192]{3,2,1,0:T(8,128)} copy(f32[1,4,192,192]{3,1,2,0:T(4,128)} %bitcast.44) | data formatting | bytes 1179648 | tf_op jit(solution)/shard_map/all_to_all | solution.py:63
  139.5 4.2 %all-to-all-start.2 = ((f32[8,96,192]{2,1,0:T(8,128)}), f32[8,96,192]{2,1,0:T(8,128)}, u32[]{:S(2)}, u32[]{:S(2)}) async-start(f32[8,96,192]{2,1,0:T(8,128)} %bitcast.43), calls=%async_computation.2 | async-start | bytes 1572864 | tf_op jit(solution)/shard_map/all_to_all | solution.py:66
  143.7 0.0 copy-done.5
  143.7 6.2 %psum.23 = f32[4,96]{1,0:T(4,128)S(1)} all-reduce(f32[4,96]{1,0:T(4,128)S(1)} %bitcast.49), channel_id=1, replica_groups=mesh['shard'=8,'tensor'=4] {'tensor'}, use_global_device_ids=true, to_apply=%region_5.6 | all-reduce | flops 384 | bytes 3072 | tf_op jit(solution)/shard_map/psum | solution.py:42
  150.0 0.0 copy-done.6
  150.0 0.0 copy-done.7
  150.0 0.6 add_divide_fusion
  150.6 0.0 copy-start.3
  150.6 2.1 %multiply_reduce_fusion.1 = (f32[4]{0:T(128)S(1)}, f32[4,96,192]{2,1,0:T(8,128)}) fusion(f32[4,96,192]{2,1,0:T(8,128)} %copy-done.2, f32[4,96,192]{2,1,0:T(8,128)} %param.11), kind=kLoop, calls=%fused_computation.18 | loop fusion | flops 663548 | bytes 884752 | tf_op jit(solution)/shard_map/reduce_sum | solution.py:41
  152.7 4.0 %fusion.3 = f32[1,192,768]{2,1,0:T(8,128)} fusion(f32[768,768]{0,1:T(8,128)S(1)} %maximum_select_fusion, s32[]{:T(128)S(6)} %select_n.23, f32[1,192,768]{2,1,0:T(8,128)} %param.12), kind=kOutput, calls=%fused_computation.6 | convolution fusion | flops 1359396864 | bytes 4325380 | tf_op jit(solution)/shard_map/dot_general | solution.py:54
  156.7 0.0 copy-done.3
  156.7 4.8 %fusion.1 = f32[1,192,768]{2,1,0:T(8,128)} fusion(f32[768,192]{1,0:T(8,128)S(1)} %bitcast.41, f32[768,768]{0,1:T(8,128)S(1)} %maximum_select_fusion, f32[1,192,768]{2,1,0:T(8,128)S(1)} %copy-done.3), kind=kOutput, calls=%fused_computation.3 | convolution fusion | flops 1359396864 | bytes 4128768 | tf_op jit(solution)/shard_map/dot_general | solution.py:57
  161.5 2.4 %all-to-all-done.2 = f32[8,96,192]{2,1,0:T(8,128)} async-done(((f32[8,96,192]{2,1,0:T(8,128)}), f32[8,96,192]{2,1,0:T(8,128)}, u32[]{:S(2)}, u32[]{:S(2)}) %all-to-all-start.2) | async-done | bytes 589856 | tf_op jit(solution)/shard_map/all_to_all | solution.py:66
  163.9 1.4 reshape.36
  165.3 0.3 dot_general.32
  165.7 1.1 multiply_reduce_fusion
  166.8 38.0 %all-reduce = (f32[4]{0:T(128)S(1)}, f32[4]{0:T(128)S(1)}) all-reduce(f32[4]{0:T(128)S(1)} %get-tuple-element.42, f32[4]{0:T(128)S(1)} %get-tuple-element.40), channel_id=1, replica_groups=mesh['shard'=8,'tensor'=4] {'shard','tensor'}, use_global_device_ids=true, to_apply=%region_4.5 | all-reduce | flops 8 | bytes 64 | tf_op jit(solution)/shard_map/psum | solution.py:76
  204.8 0.1 broadcast_multiply_fusion
  205.0 0.8 copy.36
  (1 shorter events, 0.0 us)
Async XLA Ops:
  7.2 100.4 %copy-start = (bf16[1,192,768]{2,1,0:T(8,128)(2,1)S(1)}, bf16[1,192,768]{2,1,0:T(8,128)(2,1)}, u32[]{:S(2)}) copy-start(bf16[1,192,768]{2,1,0:T(8,128)(2,1)} %param.14) | copy-start | bytes 884740
  7.2 32.2 %reduce-scatter.4.cloned.1.call-start = ((), (), s32[]{:S(2)}) async-start(), calls=%async_computation.5 | async-start | bytes 1474560
  10.8 30.5 %copy-start.4 = (s32[4]{0:T(128)S(1)}, s32[4]{0:T(128)}, u32[]{:S(2)}) copy-start(s32[4]{0:T(128)} %param.16) | copy-start | bytes 52
  10.8 99.0 %all-gather.3.cloned.1.call-start = ((), (), s32[]{:S(2)}) async-start(), calls=%async_computation.4 | async-start | bytes 1474560 | tf_op jit(solution)/shard_map/all_gather | solution.py:60
  40.8 1.3 copy-start.2
  68.2 2.1 collective-permute-start
  70.3 1.0 copy-start.1
  70.3 34.5 %collective-permute-start.1 = (f32[768,384]{0,1:T(8,128)S(1)}, f32[768,384]{0,1:T(8,128)}, u32[]{:S(2)}, u32[]{:S(2)}) collective-permute-start(f32[768,384]{0,1:T(8,128)S(1)} %maximum_select_fusion.1), channel_id=1, source_target_pairs={{0,2},{1,3},{2,0},{3,1},{4,6},{5,7},{6,4},{7,5},{8,10},{9,11},{10,... | collective-permute-start | bytes 3538952 | tf_op jit(solution)/shard_map/ppermute | solution.py:20
  134.8 9.0 %copy-start.5 = (f32[1,4,96]{2,1,0:T(4,128)S(1)}, f32[1,4,96]{2,1,0:T(4,128)}, u32[]{:S(2)}) copy-start(f32[1,4,96]{2,1,0:T(4,128)} %param.17) | copy-start | bytes 4612
  134.8 15.2 %copy-start.6 = (f32[4,96]{1,0:T(4,128)S(1)}, f32[4,96]{1,0:T(4,128)}, u32[]{:S(2)}) copy-start(f32[4,96]{1,0:T(4,128)} %param.19) | copy-start | bytes 4612
  134.8 15.2 %copy-start.7 = (f32[4,96]{1,0:T(4,128)S(1)}, f32[4,96]{1,0:T(4,128)}, u32[]{:S(2)}) copy-start(f32[4,96]{1,0:T(4,128)} %param.18) | copy-start | bytes 4612
  139.5 24.4 %all-to-all-start.2 = ((f32[8,96,192]{2,1,0:T(8,128)}), f32[8,96,192]{2,1,0:T(8,128)}, u32[]{:S(2)}, u32[]{:S(2)}) async-start(f32[8,96,192]{2,1,0:T(8,128)} %bitcast.43), calls=%async_computation.2 | async-start | bytes 1572864 | tf_op jit(solution)/shard_map/all_to_all | solution.py:66
  150.6 6.1 %copy-start.3 = (f32[1,192,768]{2,1,0:T(8,128)S(1)}, f32[1,192,768]{2,1,0:T(8,128)}, u32[]{:S(2)}) copy-start(f32[1,192,768]{2,1,0:T(8,128)} %param.13) | copy-start | bytes 1769476
Sparse Core Ops, SparseCore 0:
  10.9 28.4 reduce-scatter.3
  68.4 22.1 all-gather.2
